TPU v7x, 256 devices: a whole 4x4x8 slice. The times are simulated.
256 devices in a mesh: tiles: 32 (over z, x), sub: 8 (over y, core).
Axes of the slice: x: 4, y: 4, z: 8, core: 2. Of those that a mesh axis runs over, the one named last changes fastest.
Arguments:
- latents: float32 [196608, 512], P(('tiles', 'sub')), may hold values from -130 to 130
- conv_weight: float32 [512, 9, 512], P('tiles'), may hold values from -0.09375 to 0.09375
- conv_bias: float32 [512], replicated, may hold values from -4 to 4
- norm1_gain: float32 [512], replicated, may hold values from 0.5 to 1.5
- norm1_shift: float32 [512], replicated, may hold values from -3 to 3
- norm2_gain: float32 [512], replicated, may hold values from 0.5 to 1.5
- norm2_shift: float32 [512], replicated, may hold values from -3 to 3
- tile_counts: int32 [36], replicated, may hold values from 1 to 64, 768 in all
- widths: int32 [36], replicated, may hold values from 32 to 128, as said below
Outputs:
- activated: float32 [196608, 512], P(('tiles', 'sub'))
Inputs may be any that keep to these rules, and one draw needn't show every extreme that they name: `widths`: each width is 128, 64 or 32; some image has width 128 and some has width 128 / 4. `tile_counts`: they add up to 768; the largest is 64.
All inputs are finite; a program needn't handle non-finite values.
Results may differ from a plain program's by a relative error of at most 0.00014.
Values sent between devices are 32-bit elements; how exact they have to be, the bound alone decides.
A program may use at most 128 MiB of HBM per device.

v0:
```python
import jax
import jax.numpy as jnp
from jax import lax
from jax.sharding import PartitionSpec as P

GROUPS = 32
WMAX = 128
TILE = 256
epsilon = 1e-06
highest = lax.Precision.HIGHEST


def extended(cells, sides, width):
    for axis, dim in sides:
        count = lax.axis_size(axis)
        ends = count - 1
        head = lax.slice_in_dim(cells, 0, width, axis=dim)
        tail = lax.slice_in_dim(cells, cells.shape[dim] - width, cells.shape[dim], axis=dim)
        cells = jnp.concatenate(
            [
                lax.ppermute(tail, axis, [(i, (i + 1) % count) for i in range(ends)]),
                cells,
                lax.ppermute(head, axis, [((i + 1) % count, i) for i in range(ends)]),
            ],
            axis=dim,
        )
    return cells


def pixel_layout(tile_counts, widths, pixels_here):
    device = lax.axis_index("tiles") * lax.axis_size("sub") + lax.axis_index("sub")
    pixel_counts = tile_counts * TILE
    image_ends = jnp.cumsum(pixel_counts)
    image_starts = image_ends - pixel_counts
    position = device * pixels_here + jnp.arange(pixels_here, dtype=jnp.int32)
    member = (position[None, :] >= image_starts[:, None]) & (
        position[None, :] < image_ends[:, None]
    )

    def per_pixel(per_image):
        return jnp.sum(jnp.where(member, per_image[:, None], 0), axis=0)

    pixel_width = per_pixel(widths)
    offset = position - per_pixel(image_starts)
    row_index = offset // pixel_width
    column_index = offset - row_index * pixel_width
    pixel_height = per_pixel(pixel_counts) // pixel_width
    return (
        member.astype(jnp.float32),
        pixel_counts,
        row_index,
        column_index,
        pixel_width,
        pixel_height,
    )


def group_table(per_channel):
    return jnp.sum(per_channel.reshape(per_channel.shape[0], GROUPS, -1), axis=2)


def spread_rows(onehot, per_image):
    return lax.dot_general(
        onehot,
        per_image,
        (((0,), (0,)), ((), ())),
        precision=highest,
        preferred_element_type=jnp.float32,
    )


def normalize(values, norm_gain, norm_shift, onehot, pixel_counts):
    group_size = values.shape[1] // GROUPS
    entries = (pixel_counts * group_size).astype(jnp.float32)[:, None]
    firsts = jnp.dot(onehot, values, precision=highest, preferred_element_type=jnp.float32)
    group_total = lax.psum(group_table(firsts), ("tiles", "sub"))
    group_mean = group_total / entries
    centred = values - spread_rows(onehot, jnp.repeat(group_mean, group_size, axis=1))
    seconds = jnp.dot(
        onehot, centred * centred, precision=highest, preferred_element_type=jnp.float32
    )
    spread = lax.psum(group_table(seconds), ("tiles", "sub")) / entries
    inverse = spread_rows(onehot, jnp.repeat(lax.rsqrt(spread + epsilon), group_size, axis=1))
    return jax.nn.silu(centred * inverse * norm_gain + norm_shift)


def shards(
    latents,
    conv_weight,
    conv_bias,
    norm1_gain,
    norm1_shift,
    norm2_gain,
    norm2_shift,
    tile_counts,
    widths,
):
    pixels_here = latents.shape[0]
    channels = latents.shape[1]
    onehot, pixel_counts, row_index, column_index, pixel_width, pixel_height = pixel_layout(
        tile_counts, widths, pixels_here
    )
    first_act = normalize(latents, norm1_gain, norm1_shift, onehot, pixel_counts)
    padded = extended(first_act.T, ((("tiles", "sub"), 1),), WMAX + 1)
    anchor = jnp.arange(pixels_here, dtype=jnp.int32) + (WMAX + 1)
    sources = []
    validity = []
    for step_y in (-1, 0, 1):
        for step_x in (-1, 0, 1):
            inside = (row_index + step_y >= 0) & (row_index + step_y < pixel_height)
            inside = inside & (column_index + step_x >= 0) & (column_index + step_x < pixel_width)
            sources.append(jnp.where(inside, anchor + step_y * pixel_width + step_x, anchor))
            validity.append(inside.astype(jnp.float32))
    all_sources = jnp.concatenate(sources)
    all_masks = jnp.concatenate(validity)
    tapped = jnp.take(padded, all_sources, axis=1) * all_masks[None, :]
    zero_sum = jnp.zeros((pixels_here, channels), jnp.float32)
    running = zero_sum
    weight_piece = lax.all_gather(conv_weight, "tiles", axis=0, tiled=True)
    row_count = weight_piece.shape[0]
    block_width = min(row_count, 128)
    for block_start in range(0, row_count, block_width):
        block_rows = min(block_width, row_count - block_start)
        taps_block = lax.dynamic_slice_in_dim(tapped, block_start, block_rows, 0)
        taps_block = taps_block.reshape(block_rows, 9, pixels_here)
        weight_block = weight_piece[block_start : block_start + block_rows]
        running = running + jnp.einsum(
            "ktp,kto->po",
            taps_block,
            weight_block,
            precision=highest,
            preferred_element_type=jnp.float32,
        )
    hidden = running
    hidden = hidden + conv_bias
    return normalize(hidden, norm2_gain, norm2_shift, onehot, pixel_counts)


def solution(mesh):
    return jax.shard_map(
        shards,
        mesh=mesh,
        in_specs=(
            P(("tiles", "sub"), None),
            P("tiles", None, None),
            P(),
            P(),
            P(),
            P(),
            P(),
            P(),
            P(),
        ),
        out_specs=P(("tiles", "sub"), None),
        check_vma=False,
    )
```

profile of v0, /device:TPU:1, one launch (start us, length us, event | category | flops | bytes accessed | tf_op | source)
XLA Modules:
  0.0 427.4 jit_solution(8447993397408596706)
XLA Ops:
  6.5 0.7 all-gather.2.cloned.1.call-update
  7.3 0.7 broadcast_multiply_fusion
  8.2 0.7 fusion.25
  8.9 2.8 bitcast_reduce_fusion.3
  11.7 83.9 %psum.28 = f32[36,32]{0,1:T(8,128)S(1)} all-reduce(f32[36,32]{0,1:T(8,128)S(1)} %bitcast_reduce_fusion.3), channel_id=1, replica_groups=mesh['tiles'=32,'sub'=8] {'tiles','sub'}, use_global_device_ids=true, to_apply=%region_5.6 | all-reduce | flops 1152 | bytes 9216 | tf_op jit(solution)/shard_map/psum | solution.py:76
  95.6 0.9 convolution_subtract_fusion.1
  96.6 1.4 bitcast_reduce_fusion.2
  98.0 73.4 %psum.29 = f32[36,32]{0,1:T(8,128)S(1)} all-reduce(f32[36,32]{0,1:T(8,128)S(1)} %bitcast_reduce_fusion.2), channel_id=1, replica_groups=mesh['tiles'=32,'sub'=8] {'tiles','sub'}, use_global_device_ids=true, to_apply=%region_7.8 | all-reduce | flops 1152 | bytes 9216 | tf_op jit(solution)/shard_map/psum | solution.py:82
  171.5 1.3 multiply_bitcast_fusion.1
  172.8 1.1 copy-done.4
  174.0 3.2 collective-permute-start
  177.2 2.4 collective-permute-start.1
  179.9 0.2 dynamic-update-slice
  180.1 0.2 dynamic-update-slice.1
  180.8 0.2 dynamic-update-slice.3
  181.3 0.2 dynamic-update-slice.5
  181.6 0.2 dynamic-update-slice.6
  182.4 2.6 collective-permute-done.1
  185.0 4.5 %concatenate.54 = f32[512,1026]{0,1:T(8,128)S(1)} concatenate(f32[512,129]{0,1:T(8,128)S(1)} %collective-permute-done, f32[512,768]{0,1:T(8,128)} %copy-done.4, f32[512,129]{0,1:T(8,128)S(1)} %collective-permute-done.1), dimensions={1} | concatenate | bytes 4202496 | tf_op jit(solution)/shard_map/concatenate | solution.py:19
  189.5 18.6 %gather_fusion = f32[6912,512]{1,0:T(8,128)} fusion(f32[512,1026]{0,1:T(8,128)S(1)} %concatenate.54, s32[7168]{0:T(1024)S(1)} %pad_clamp_fusion), kind=kCustom, calls=%fused_computation | custom fusion | bytes 28339200 | tf_op jit(solution)/shard_map/jit(_take)/gather | solution.py:116
  208.1 11.6 %multiply_bitcast_fusion = f32[512,6912]{0,1:T(8,128)} fusion(f32[6912,512]{1,0:T(8,128)} %gather_fusion, f32[6912]{0:T(1024)S(1)} %concatenate.66, pred[6912]{0:T(1024)(128)(4,1)S(1)} %compare_and_fusion.1), kind=kLoop, calls=%fused_computation.1 | loop fusion | flops 7077888 | bytes 28346112 | tf_op jit(solution)/shard_map/mul | solution.py:116
  219.7 9.4 %fusion.35 = (f32[128,6912]{0,1:T(8,128)}, f32[128,6912]{0,1:T(8,128)}, f32[128,6912]{0,1:T(8,128)}, f32[128,6912]{0,1:T(8,128)S(1)}) fusion(f32[512,6912]{0,1:T(8,128)} %multiply_bitcast_fusion), kind=kLoop, calls=%fused_computation.106 | loop fusion | bytes 28311552 | tf_op jit(solution)/shard_map/dynamic_slice | solution.py:124
  229.1 9.2 %fusion = f32[768,512,1]{1,0,2:T(8,128)S(1)} fusion(f32[128,9,768]{0,2,1:T(8,128)} %bitcast.48, f32[512,9,512]{2,0,1:T(8,128)} %all-gather.2.cloned.1.call-done), kind=kOutput, calls=%fused_computation.2 | convolution fusion | flops 5435817984 | bytes 7471104 | tf_op jit(solution)/shard_map/ktp,kto->po/dot_general | solution.py:127
  238.2 8.0 %fusion.2 = f32[768,512,1]{1,0,2:T(8,128)S(1)} fusion(f32[128,9,768]{0,2,1:T(8,128)S(1)} %bitcast.47, f32[512,9,512]{2,0,1:T(8,128)} %all-gather.2.cloned.1.call-done), kind=kOutput, calls=%fused_computation.4 | convolution fusion | flops 5435817984 | bytes 7471104 | tf_op jit(solution)/shard_map/ktp,kto->po/dot_general | solution.py:127
  246.3 6.5 %fusion.4 = f32[768,512,1]{1,0,2:T(8,128)S(1)} fusion(f32[128,9,768]{0,2,1:T(8,128)S(1)} %bitcast.46, f32[512,9,512]{2,0,1:T(8,128)S(1)} %copy-done.2), kind=kOutput, calls=%fused_computation.6 | convolution fusion | flops 5435817984 | bytes 7471104 | tf_op jit(solution)/shard_map/ktp,kto->po/dot_general | solution.py:127
  252.8 6.4 %fusion.8 = f32[768,512]{1,0:T(8,128)S(1)} fusion(f32[768,512,1]{1,0,2:T(8,128)S(1)} %fusion, f32[768,512,1]{1,0,2:T(8,128)S(1)} %fusion.2, f32[768,512,1]{1,0,2:T(8,128)S(1)} %fusion.4, f32[128,9,768]{0,2,1:T(8,128)S(1)} %bitcast.49, f32[512,9,512]{2,0,1:T(8,128)S(1)} %copy-done.2, f32[512]{0:T(512)S(1)} %copy-done.5), kind=kOutput, calls=%fused_computation.11 | convolution fusion | flops 5437390848 | bytes 12191744 | tf_op jit(solution)/shard_map/ktp,kto->po/dot_general | solution.py:127
  259.2 1.4 bitcast_reduce_fusion.1
  260.6 82.0 %psum.30 = f32[36,32]{0,1:T(8,128)S(1)} all-reduce(f32[36,32]{0,1:T(8,128)S(1)} %bitcast_reduce_fusion.1), channel_id=1, replica_groups=mesh['tiles'=32,'sub'=8] {'tiles','sub'}, use_global_device_ids=true, to_apply=%region_9.10 | all-reduce | flops 1152 | bytes 9216 | tf_op jit(solution)/shard_map/psum | solution.py:76
  342.6 0.9 convolution_subtract_fusion
  343.6 1.4 bitcast_reduce_fusion
  345.0 72.8 %psum.31 = f32[36,32]{0,1:T(8,128)S(1)} all-reduce(f32[36,32]{0,1:T(8,128)S(1)} %bitcast_reduce_fusion), channel_id=1, replica_groups=mesh['tiles'=32,'sub'=8] {'tiles','sub'}, use_global_device_ids=true, to_apply=%region_11.12 | all-reduce | flops 1152 | bytes 9216 | tf_op jit(solution)/shard_map/psum | solution.py:82
  417.9 2.4 divide_multiply_fusion
  (69 shorter events, 2.0 us)
Async XLA Ops:
  6.5 89.1 %copy-start.3 = (f32[768,512]{1,0:T(8,128)S(1)}, f32[768,512]{1,0:T(8,128)}, u32[]{:S(2)}) copy-start(f32[768,512]{1,0:T(8,128)} %param.9) | copy-start | bytes 4718596
  6.5 222.5 %all-gather.2.cloned.1.call-start = ((), (), s32[]{:S(2)}) async-start(), calls=%async_computation | async-start | bytes 9732096 | tf_op jit(solution)/shard_map/all_gather | solution.py:119
  96.6 74.9 %copy-start.7 = (f32[512]{0:T(512)S(1)}, f32[512]{0:T(512)}, u32[]{:S(2)}) copy-start(f32[512]{0:T(512)} %param.13) | copy-start | bytes 6148
  96.6 74.9 %copy-start.8 = (f32[512]{0:T(512)S(1)}, f32[512]{0:T(512)}, u32[]{:S(2)}) copy-start(f32[512]{0:T(512)} %param.12) | copy-start | bytes 6148
  171.5 8.1 %copy-start.6 = (s32[36]{0:T(128)S(1)}, s32[36]{0:T(128)}, u32[]{:S(2)}) copy-start(s32[36]{0:T(128)} %param.17) | copy-start | bytes 436
  172.8 1.1 copy-start.4
  174.0 8.5 %collective-permute-start = (f32[512,129]{0,1:T(8,128)S(1)}, f32[512,129]{0,1:T(8,128)S(1)}, u32[]{:S(2)}, u32[]{:S(2)}) collective-permute-start(f32[512,129]{0,1:T(8,128)S(1)} %get-tuple-element.44), channel_id=1, source_target_pairs={{0,1},{1,2},{2,3},{3,4},{4,5},{5,6},{6,7},{7,8},{8,9},{9,10},{10,1... | collective-permute-start | bytes 792584 | tf_op jit(solution)/shard_map/ppermute | solution.py:21
  177.2 7.9 %collective-permute-start.1 = (f32[512,129]{0,1:T(8,128)S(1)}, f32[512,129]{0,1:T(8,128)S(1)}, u32[]{:S(2)}, u32[]{:S(2)}) collective-permute-start(f32[512,129]{0,1:T(8,128)S(1)} %get-tuple-element.43), channel_id=1, source_target_pairs={{1,0},{2,1},{3,2},{4,3},{5,4},{6,5},{7,6},{8,7},{9,8},{10,9},{11,1... | collective-permute-start | bytes 792584 | tf_op jit(solution)/shard_map/ppermute | solution.py:23
  229.1 9.2 %copy-start = (f32[128,6912]{0,1:T(8,128)S(1)}, f32[128,6912]{0,1:T(8,128)}, u32[]{:S(2)}) copy-start(f32[128,6912]{0,1:T(8,128)} %get-tuple-element.41) | copy-start | bytes 10616836
  229.1 17.2 %copy-start.2 = (f32[512,9,512]{2,0,1:T(8,128)S(1)}, f32[512,9,512]{2,0,1:T(8,128)}, u32[]{:S(2)}) copy-start(f32[512,9,512]{2,0,1:T(8,128)} %all-gather.2.cloned.1.call-done) | copy-start | bytes 28311556
  246.2 6.5 %copy-start.1 = (f32[128,6912]{0,1:T(8,128)S(1)}, f32[128,6912]{0,1:T(8,128)}, u32[]{:S(2)}) copy-start(f32[128,6912]{0,1:T(8,128)} %get-tuple-element.39) | copy-start | bytes 10616836
  246.3 6.5 %copy-start.5 = (f32[512]{0:T(512)S(1)}, f32[512]{0:T(512)}, u32[]{:S(2)}) copy-start(f32[512]{0:T(512)} %param.11) | copy-start | bytes 6148
  343.6 74.3 %copy-start.9 = (f32[512]{0:T(512)S(1)}, f32[512]{0:T(512)}, u32[]{:S(2)}) copy-start(f32[512]{0:T(512)} %param.15) | copy-start | bytes 6148
  343.6 74.3 %copy-start.10 = (f32[512]{0:T(512)S(1)}, f32[512]{0:T(512)}, u32[]{:S(2)}) copy-start(f32[512]{0:T(512)} %param.14) | copy-start | bytes 6148
Sparse Core Ops, SparseCore 0:
  9.9 107.2 all-gather.1
where the time goes:
time: 433 us; the launch traced here: 427 us
  blocking collectives  312 us (72%)
  matrix products  42.7 us (10%)
  local copies, waits for them, and re-layouts  35.8 us (8%)
  between operations  14 us (3%)
  other arithmetic  13.9 us (3%)
  starting transfers between devices  5.59 us (1%)
    psum x2, blocking collectives, normalize(): group_total = lax.psum(group_table(firsts), ('tiles', 'sub'))  166 us
    psum x2, blocking collectives, normalize(): spread = lax.psum(group_table(seconds), ('tiles', 'sub')) / entries  146 us
    dot_general x4, matrix products, shards(): jnp.einsum('ktp,kto->po', taps_block, weight_block, precision=highest, pr...  30 us
    gather x1, local copies, waits for them, and re-layouts, shards(): tapped = jnp.take(padded, all_sources, axis=1) * all_masks[None, :]  18.6 us
    mul x1, other arithmetic, shards(): tapped = jnp.take(padded, all_sources, axis=1) * all_masks[None, :]  11.6 us
    dynamic_slice x1, local copies, waits for them, and re-layouts, shards(): taps_block = lax.dynamic_slice_in_dim(tapped, block_start, block_rows, 0)  9.35 us
  transfers between devices with their start and end apart: 3, of which 1 were waited for; matrix products, arithmetic and copies ran while one was open for 13% of the time, Pallas kernels for 0%

commit v1 on v0

--- a/solution.py
+++ b/solution.py
@@ -8,6 +8,12 @@
 TILE = 256
 epsilon = 1e-06
 highest = lax.Precision.HIGHEST
+
+
+def summed_here(array, name):
+    parts = lax.all_gather(array, name, axis=0, tiled=False)
+    total = parts.sum(axis=0)
+    return total
 
 
 def extended(cells, sides, width):
@@ -73,7 +79,7 @@
     group_size = values.shape[1] // GROUPS
     entries = (pixel_counts * group_size).astype(jnp.float32)[:, None]
     firsts = jnp.dot(onehot, values, precision=highest, preferred_element_type=jnp.float32)
-    group_total = lax.psum(group_table(firsts), ("tiles", "sub"))
+    group_total = summed_here(group_table(firsts), ("tiles", "sub"))
     group_mean = group_total / entries
     centred = values - spread_rows(onehot, jnp.repeat(group_mean, group_size, axis=1))
     seconds = jnp.dot(

time: 433 us -> 526 us (1.21)
  waiting for transfers between devices: 3.31 us -> 237 us
  blocking collectives: 312 us -> 153 us
  local copies, waits for them, and re-layouts: 35.8 us -> 44 us
  other arithmetic: 13.9 us -> 20.7 us
    all_gather x0 -> x2, waiting for transfers between devices: none -> 231 us  [summed_here(): parts = lax.all_gather(array, name, axis=0, tiled=False)]
    psum x2 -> x0, blocking collectives: 166 us -> none  [normalize(): group_total = lax.psum(group_table(firsts), ('tiles', 'sub'))]
    unnamed x38, local copies, waits for them, and re-layouts: 3.19 us -> 11.4 us
    psum x2, blocking collectives: 146 us -> 153 us  [normalize(): spread = lax.psum(group_table(seconds), ('tiles', 'sub')) / entries]
  transfers between devices with their start and end apart: 3 -> 5, of which waited for: 1 -> 4; matrix products, arithmetic and copies ran while one was open for 13% -> 12% of each run, Pallas kernels for 0% -> 0%
where the time goes in v1:
time: 526 us; the launch traced here: 517 us
  waiting for transfers between devices  237 us (45%)
  blocking collectives  153 us (29%)
  matrix products  44.1 us (8%)
  local copies, waits for them, and re-layouts  44 us (8%)
  other arithmetic  20.7 us (4%)
  between operations  13.7 us (3%)
    all_gather x2, waiting for transfers between devices, summed_here(): parts = lax.all_gather(array, name, axis=0, tiled=False)  231 us
    psum x2, blocking collectives, normalize(): spread = lax.psum(group_table(seconds), ('tiles', 'sub')) / entries  153 us
    dot_general x4, matrix products, shards(): jnp.einsum('ktp,kto->po', taps_block, weight_block, precision=highest, pr...  30 us
    gather x1, local copies, waits for them, and re-layouts, shards(): tapped = jnp.take(padded, all_sources, axis=1) * all_masks[None, :]  18.6 us
    mul x1, other arithmetic, shards(): tapped = jnp.take(padded, all_sources, axis=1) * all_masks[None, :]  12.1 us
    unnamed x38, local copies, waits for them, and re-layouts  11.4 us
  transfers between devices with their start and end apart: 5, of which 4 were waited for; matrix products, arithmetic and copies ran while one was open for 12% of the time, Pallas kernels for 0%

profile of v1, /device:TPU:1, one launch (start us, length us, event | category | flops | bytes accessed | tf_op | source)
XLA Modules:
  0.0 517.4 jit_solution(6417820005132604436)
XLA Ops:
  8.2 3.5 bitcast_reduce_fusion.3
  12.7 1.4 dynamic-update-slice
  14.2 1.4 dynamic-update-slice.1
  15.6 1.4 dynamic-update-slice.2
  17.2 1.4 dynamic-update-slice.3
  18.6 1.4 dynamic-update-slice.4
  20.0 1.4 dynamic-update-slice.5
  21.6 1.4 dynamic-update-slice.6
  23.0 1.4 dynamic-update-slice.7
  25.2 106.5 %all-gather.10.cloned.1.call-done = f32[256,36,32]{1,2,0:T(8,128)} async-done(((f32[1,36,32]{1,2,0:T(8,128)}), f32[256,36,32]{1,2,0:T(8,128)}) %all-gather.10.cloned.1.call-update) | async-done | bytes 1179664 | tf_op jit(solution)/shard_map/all_gather | solution.py:14
  131.7 2.5 reduce_sum.85
  135.2 1.4 bitcast_reduce_fusion.2
  136.7 77.5 %psum.14 = f32[36,32]{0,1:T(8,128)S(1)} all-reduce(f32[36,32]{0,1:T(8,128)S(1)} %bitcast_reduce_fusion.2), channel_id=1, replica_groups=mesh['tiles'=32,'sub'=8] {'tiles','sub'}, use_global_device_ids=true, to_apply=%region_7.8 | all-reduce | flops 1152 | bytes 9216 | tf_op jit(solution)/shard_map/psum | solution.py:88
  214.3 1.3 multiply_bitcast_fusion.1
  215.6 3.2 collective-permute-start
  218.8 1.9 collective-permute-start.1
  222.3 4.8 collective-permute-done.1
  227.1 4.5 concatenate.54
  231.6 18.6 %gather_fusion = f32[6912,512]{1,0:T(8,128)} fusion(f32[512,1026]{0,1:T(8,128)S(1)} %concatenate.54, s32[7168]{0:T(1024)S(1)} %pad_clamp_fusion), kind=kCustom, calls=%fused_computation | custom fusion | bytes 28339200 | tf_op jit(solution)/shard_map/jit(_take)/gather | solution.py:122
  250.1 12.1 %multiply_bitcast_fusion = f32[512,6912]{0,1:T(8,128)} fusion(f32[6912,512]{1,0:T(8,128)} %gather_fusion, f32[6912]{0:T(1024)S(1)} %concatenate.66, pred[6912]{0:T(1024)(128)(4,1)S(1)} %compare_and_fusion.1), kind=kLoop, calls=%fused_computation.1 | loop fusion | flops 7077888 | bytes 28346112 | tf_op jit(solution)/shard_map/mul | solution.py:122
  262.2 9.4 %fusion.35 = (f32[128,6912]{0,1:T(8,128)}, f32[128,6912]{0,1:T(8,128)}, f32[128,6912]{0,1:T(8,128)}, f32[128,6912]{0,1:T(8,128)S(1)}) fusion(f32[512,6912]{0,1:T(8,128)} %multiply_bitcast_fusion), kind=kLoop, calls=%fused_computation.106 | loop fusion | bytes 28311552 | tf_op jit(solution)/shard_map/dynamic_slice | solution.py:130
  271.6 9.2 %fusion = f32[768,512,1]{1,0,2:T(8,128)S(1)} fusion(f32[128,9,768]{0,2,1:T(8,128)} %bitcast.50, f32[512,9,512]{2,0,1:T(8,128)} %all-gather.8.cloned.1.call-done), kind=kOutput, calls=%fused_computation.2 | convolution fusion | flops 5435817984 | bytes 7471104 | tf_op jit(solution)/shard_map/ktp,kto->po/dot_general | solution.py:133
  280.7 8.0 %fusion.2 = f32[768,512,1]{1,0,2:T(8,128)S(1)} fusion(f32[128,9,768]{0,2,1:T(8,128)S(1)} %bitcast.49, f32[512,9,512]{2,0,1:T(8,128)} %all-gather.8.cloned.1.call-done), kind=kOutput, calls=%fused_computation.4 | convolution fusion | flops 5435817984 | bytes 7471104 | tf_op jit(solution)/shard_map/ktp,kto->po/dot_general | solution.py:133
  288.8 6.5 %fusion.4 = f32[768,512,1]{1,0,2:T(8,128)S(1)} fusion(f32[128,9,768]{0,2,1:T(8,128)S(1)} %bitcast.48, f32[512,9,512]{2,0,1:T(8,128)S(1)} %copy-done.2), kind=kOutput, calls=%fused_computation.6 | convolution fusion | flops 5435817984 | bytes 7471104 | tf_op jit(solution)/shard_map/ktp,kto->po/dot_general | solution.py:133
  295.3 6.4 %fusion.8 = f32[768,512]{1,0:T(8,128)S(1)} fusion(f32[768,512,1]{1,0,2:T(8,128)S(1)} %fusion, f32[768,512,1]{1,0,2:T(8,128)S(1)} %fusion.2, f32[768,512,1]{1,0,2:T(8,128)S(1)} %fusion.4, f32[128,9,768]{0,2,1:T(8,128)S(1)} %bitcast.51, f32[512,9,512]{2,0,1:T(8,128)S(1)} %copy-done.2, f32[512]{0:T(512)S(1)} %copy-done.5), kind=kOutput, calls=%fused_computation.11 | convolution fusion | flops 5437390848 | bytes 12191744 | tf_op jit(solution)/shard_map/ktp,kto->po/dot_general | solution.py:133
  301.7 2.1 bitcast_reduce_fusion.1
  303.7 124.0 %all-gather.12.cloned.1.call-done = f32[256,36,32]{1,2,0:T(8,128)} async-done(((f32[1,36,32]{1,2,0:T(8,128)}), f32[256,36,32]{1,2,0:T(8,128)}) %all-gather.12.cloned.1.call-update) | async-done | bytes 1179664 | tf_op jit(solution)/shard_map/all_gather | solution.py:14
  427.8 2.5 reduce_sum.88
  430.3 1.1 convolution_subtract_fusion
  431.5 1.4 bitcast_reduce_fusion
  433.0 75.2 %psum.15 = f32[36,32]{0,1:T(8,128)S(1)} all-reduce(f32[36,32]{0,1:T(8,128)S(1)} %bitcast_reduce_fusion), channel_id=1, replica_groups=mesh['tiles'=32,'sub'=8] {'tiles','sub'}, use_global_device_ids=true, to_apply=%region_11.12 | all-reduce | flops 1152 | bytes 9216 | tf_op jit(solution)/shard_map/psum | solution.py:88
  508.2 2.4 divide_multiply_fusion
  (75 shorter events, 6.5 us)
Async XLA Ops:
  6.5 5.9 %copy-start.6 = (s32[36]{0:T(128)S(1)}, s32[36]{0:T(128)}, u32[]{:S(2)}) copy-start(s32[36]{0:T(128)} %param.17) | copy-start | bytes 436
  6.5 125.2 %all-gather.10.cloned.1.call-start = ((), (), s32[]{:S(2)}) async-start(), calls=%async_computation.1 | async-start | bytes 4210688 | tf_op jit(solution)/shard_map/all_gather | solution.py:14
  11.6 259.9 %all-gather.8.cloned.1.call-start = ((), (), s32[]{:S(2)}) async-start(), calls=%async_computation | async-start | bytes 9732096 | tf_op jit(solution)/shard_map/all_gather | solution.py:125
  12.4 415.4 %all-gather.12.cloned.1.call-start = ((), (), s32[]{:S(2)}) async-start(), calls=%async_computation.2 | async-start | bytes 4210688 | tf_op jit(solution)/shard_map/all_gather | solution.py:14
  25.2 109.1 %copy-start.3 = (f32[768,512]{1,0:T(8,128)S(1)}, f32[768,512]{1,0:T(8,128)}, u32[]{:S(2)}) copy-start(f32[768,512]{1,0:T(8,128)} %param.9) | copy-start | bytes 4718596
  135.2 79.1 %copy-start.7 = (f32[512]{0:T(512)S(1)}, f32[512]{0:T(512)}, u32[]{:S(2)}) copy-start(f32[512]{0:T(512)} %param.13) | copy-start | bytes 6148
  135.2 79.1 %copy-start.8 = (f32[512]{0:T(512)S(1)}, f32[512]{0:T(512)}, u32[]{:S(2)}) copy-start(f32[512]{0:T(512)} %param.12) | copy-start | bytes 6148
  215.6 6.7 %copy-start.4 = (f32[512,768]{0,1:T(8,128)}, f32[512,768]{0,1:T(8,128)S(1)}, u32[]{:S(2)}) copy-start(f32[512,768]{0,1:T(8,128)S(1)} %multiply_bitcast_fusion.1) | copy-start | bytes 4718596
  215.6 6.6 %collective-permute-start = (f32[512,129]{0,1:T(8,128)S(1)}, f32[512,129]{0,1:T(8,128)S(1)}, u32[]{:S(2)}, u32[]{:S(2)}) collective-permute-start(f32[512,129]{0,1:T(8,128)S(1)} %get-tuple-element.44), channel_id=1, source_target_pairs={{0,1},{1,2},{2,3},{3,4},{4,5},{5,6},{6,7},{7,8},{8,9},{9,10},{10,1... | collective-permute-start | bytes 792584 | tf_op jit(solution)/shard_map/ppermute | solution.py:27
  218.8 8.3 %collective-permute-start.1 = (f32[512,129]{0,1:T(8,128)S(1)}, f32[512,129]{0,1:T(8,128)S(1)}, u32[]{:S(2)}, u32[]{:S(2)}) collective-permute-start(f32[512,129]{0,1:T(8,128)S(1)} %get-tuple-element.43), channel_id=1, source_target_pairs={{1,0},{2,1},{3,2},{4,3},{5,4},{6,5},{7,6},{8,7},{9,8},{10,9},{11,1... | collective-permute-start | bytes 792584 | tf_op jit(solution)/shard_map/ppermute | solution.py:29
  271.5 9.2 %copy-start = (f32[128,6912]{0,1:T(8,128)S(1)}, f32[128,6912]{0,1:T(8,128)}, u32[]{:S(2)}) copy-start(f32[128,6912]{0,1:T(8,128)} %get-tuple-element.41) | copy-start | bytes 10616836
  271.6 17.2 %copy-start.2 = (f32[512,9,512]{2,0,1:T(8,128)S(1)}, f32[512,9,512]{2,0,1:T(8,128)}, u32[]{:S(2)}) copy-start(f32[512,9,512]{2,0,1:T(8,128)} %all-gather.8.cloned.1.call-done) | copy-start | bytes 28311556
  288.7 6.5 %copy-start.1 = (f32[128,6912]{0,1:T(8,128)S(1)}, f32[128,6912]{0,1:T(8,128)}, u32[]{:S(2)}) copy-start(f32[128,6912]{0,1:T(8,128)} %get-tuple-element.39) | copy-start | bytes 10616836
  288.7 6.5 %copy-start.5 = (f32[512]{0:T(512)S(1)}, f32[512]{0:T(512)}, u32[]{:S(2)}) copy-start(f32[512]{0:T(512)} %param.11) | copy-start | bytes 6148
  431.5 76.7 %copy-start.9 = (f32[512]{0:T(512)S(1)}, f32[512]{0:T(512)}, u32[]{:S(2)}) copy-start(f32[512]{0:T(512)} %param.15) | copy-start | bytes 6148
  431.5 76.7 %copy-start.10 = (f32[512]{0:T(512)S(1)}, f32[512]{0:T(512)}, u32[]{:S(2)}) copy-start(f32[512]{0:T(512)} %param.14) | copy-start | bytes 6148
Sparse Core Ops, SparseCore 0:
  11.8 119.9 all-gather.9
  134.3 100.1 all-gather.7
  303.9 123.8 all-gather.11
